TPU v7x, 256 devices: a whole 4x4x8 slice. The times are simulated.
256 devices in a mesh: pix: 16 (over x_hi, z), peak: 16 (over y, x_lo, core).
Axes of the slice: x: 4 (x_hi: 2, x_lo: 2; x = x_hi * 2 + x_lo), y: 4, z: 8, core: 2. Of those that a mesh axis runs over, the one named last changes fastest.
Arguments:
- cube: bfloat16 [65536, 8, 2048], P('pix', None, 'peak'), may hold values from -6 to 6
- pix_factor: bfloat16 [65536, 64], P(('pix', 'peak')), may hold values from -0.8984375 to 0.8984375
- sec_factor: bfloat16 [8, 64], replicated, may hold values from -5 to 5
- peak_factor: bfloat16 [2048, 64], P('peak'), may hold values from -0.046875 to 0.046875
Outputs:
- grad_pix: float32 [65536, 64], P(('pix', 'peak'))
- grad_peak: float32 [2048, 64], P('peak')
All inputs are finite; a program needn't handle non-finite values.
Results may differ from a plain program's by a relative error of at most 0.0003.
Values may be sent and summed in bfloat16 or wider, within the bound.
No kernel may reach another device: no remote copies, remote signals or barrier semaphores. Data moves between devices by JAX's collectives and lax.ppermute only.
A program may use at most 64 MiB of HBM per device.

v0:
```python
import math

import jax
import jax.numpy as jnp
from jax import lax
from jax.sharding import PartitionSpec as P


def on_device(cube, pix_factor, sec_factor, peak_factor):
    pixels = cube.shape[0]
    sections = cube.shape[1]
    peaks = cube.shape[2]
    rank = peak_factor.shape[1]
    fb = sec_factor.astype(jnp.float32)
    fa_own = pix_factor.astype(jnp.float32)
    fc_own = peak_factor.astype(jnp.float32)
    gathered = lax.all_gather(pix_factor, "peak", axis=0, tiled=True)
    ttm = jnp.dot(
        cube.reshape(pixels * sections, peaks), peak_factor, preferred_element_type=jnp.float32
    )
    ttm = ttm.reshape(pixels, sections, rank)
    summed_pix = lax.psum_scatter(
        jnp.sum(ttm * fb[None, :, :], axis=1), "peak", scatter_dimension=0, tiled=True
    )
    partial_peak = jnp.zeros((peaks, rank), jnp.float32)
    for index in range(sections):
        inner = lax.dot_general(
            cube[:, index, :],
            gathered,
            (((0,), (0,)), ((), ())),
            preferred_element_type=jnp.float32,
        )
        partial_peak = partial_peak + inner * fb[index][None, :]
    local_a = jnp.dot(pix_factor.T, pix_factor, preferred_element_type=jnp.float32)
    local_c = jnp.dot(peak_factor.T, peak_factor, preferred_element_type=jnp.float32)
    gram_b = jnp.dot(sec_factor.T, sec_factor, preferred_element_type=jnp.float32)
    gram_a = lax.psum(local_a, ("pix", "peak"))
    gram_c = lax.psum(local_c, "peak")
    grad_pix = summed_pix - jnp.dot(fa_own, gram_b * gram_c, precision=lax.Precision.HIGHEST)
    scale = 1.0 / math.sqrt(float(sections * pixels * lax.axis_size("pix")))
    weight_c = gram_a * gram_b
    total = lax.psum(partial_peak, "pix")
    grad_peak = (total - jnp.dot(fc_own, weight_c, precision=lax.Precision.HIGHEST)) * scale
    return (grad_pix, grad_peak)


def solution(mesh):
    in_specs = (P("pix", None, "peak"), P(("pix", "peak"), None), P(), P("peak", None))
    out_specs = (P(("pix", "peak"), None), P("peak", None))
    return jax.shard_map(
        on_device, mesh=mesh, in_specs=in_specs, out_specs=out_specs, check_vma=False
    )
```

profile of v0, /device:TPU:2, one launch (start us, length us, event | category | flops | bytes accessed | tf_op | source)
XLA Modules:
  0.0 270.1 jit_solution(18076057092134265733)
XLA Ops:
  7.2 0.0 copy-start
  7.2 0.0 reduce-scatter.2.cloned.1.call-start
  7.2 0.7 convert_element_type.2
  7.9 0.0 copy-done
  7.9 7.9 %multiply_reduce_fusion = f32[4096,64]{0,1:T(8,128)} fusion(f32[8,64]{1,0:T(8,128)S(1)} %convert_element_type.2, bf16[128,64]{0,1:T(8,128)(2,1)S(1)} %copy-done, bf16[4096,8,128]{2,1,0:T(8,128)(2,1)} %param.4), kind=kOutput, calls=%fused_computation | convolution fusion | flops 540803072 | bytes 9455616 | tf_op jit(solution)/shard_map/dot_general | solution.py:18
  15.9 0.0 reduce-scatter.2.cloned.1.call-update
  15.9 0.0 copy-start.1
  15.9 7.7 %copy.7 = bf16[4096,8,128]{2,0,1:T(8,128)(2,1)} copy(bf16[4096,8,128]{2,1,0:T(8,128)(2,1)} %param.4) | data formatting | bytes 16777216 | tf_op args[0]
  23.6 0.0 copy-done.1
  23.6 0.0 copy-start.2
  23.6 20.3 %all_gather.3 = bf16[4096,64]{0,1:T(8,128)(2,1)S(1)} all-gather(bf16[256,64]{0,1:T(8,128)(2,1)S(1)} %copy-done.1), channel_id=1, replica_groups=mesh['pix'=16,'peak'=16] {'peak'}, dimensions={0}, use_global_device_ids=true | all-gather | bytes 557056 | tf_op jit(solution)/shard_map/all_gather | solution.py:17
  43.9 0.1 fusion.16
  44.0 0.1 fusion.15
  44.2 1.6 convolution_multiply_fusion.7
  45.7 1.5 fusion.7
  47.3 78.9 %psum.23 = f32[64,64]{1,0:T(8,128)S(1)} all-reduce(f32[64,64]{1,0:T(8,128)S(1)} %fusion.16), channel_id=1, replica_groups=mesh['pix'=16,'peak'=16] {'pix','peak'}, use_global_device_ids=true, to_apply=%region_4.0 | all-reduce | flops 4096 | bytes 32768 | tf_op jit(solution)/shard_map/psum | solution.py:37
  126.2 52.1 %psum.21 = f32[64,64]{1,0:T(8,128)S(1)} all-reduce(f32[64,64]{1,0:T(8,128)S(1)} %fusion.15), channel_id=1, replica_groups=mesh['pix'=16,'peak'=16] {'peak'}, use_global_device_ids=true, to_apply=%region_2.0 | all-reduce | flops 4096 | bytes 32768 | tf_op jit(solution)/shard_map/psum | solution.py:38
  178.3 1.5 fusion.6
  179.8 1.5 fusion.5
  181.4 1.5 fusion.4
  182.9 1.5 fusion.3
  184.5 1.5 fusion.2
  186.0 1.5 fusion.1
  187.6 73.0 %psum.22 = f32[128,64]{0,1:T(8,128)S(1)} all-reduce(f32[128,64]{0,1:T(8,128)S(1)} %fusion.1), channel_id=1, replica_groups=mesh['pix'=16,'peak'=16] {'pix'}, use_global_device_ids=true, to_apply=%region_3.0 | all-reduce | flops 8192 | bytes 65536 | tf_op jit(solution)/shard_map/psum | solution.py:42
  260.6 0.0 copy-done.2
  260.6 0.2 fusion.14
  260.8 0.8 fusion.9
  261.6 0.0 reduce-scatter.2.cloned.1.call-done
  261.6 1.7 fusion
  (1 shorter events, 0.0 us)
Async XLA Ops:
  7.2 0.8 copy-start
  7.2 254.4 %reduce-scatter.2.cloned.1.call-start = ((), (), s32[]{:S(2)}) async-start(), calls=%async_computation.1 | async-start | bytes 1114112 | tf_op jit(solution)/shard_map/reduce_scatter | solution.py:22
  15.9 7.7 %copy-start.1 = (bf16[256,64]{0,1:T(8,128)(2,1)S(1)}, bf16[256,64]{0,1:T(8,128)(2,1)}, u32[]{:S(2)}) copy-start(bf16[256,64]{0,1:T(8,128)(2,1)} %param.5) | copy-start | bytes 98308
  23.6 237.0 %copy-start.2 = (bf16[8,64]{1,0:T(8,128)(2,1)S(1)}, bf16[8,64]{1,0:T(8,128)(2,1)}, u32[]{:S(2)}) copy-start(bf16[8,64]{1,0:T(8,128)(2,1)} %param.6) | copy-start | bytes 3076
Sparse Core Ops, SparseCore 0:
  16.0 63.3 reduce-scatter.1
where the time goes:
time: 274 us; the launch traced here: 270 us
  blocking collectives  224 us (82%)
  matrix products  23.3 us (9%)
  between operations  14.1 us (5%)
  local copies, waits for them, and re-layouts  7.72 us (3%)
    psum x1, blocking collectives, on_device(): gram_a = lax.psum(local_a, ('pix', 'peak'))  78.9 us
    psum x1, blocking collectives, on_device(): total = lax.psum(partial_peak, 'pix')  73 us
    psum x1, blocking collectives, on_device(): gram_c = lax.psum(local_c, 'peak')  52.1 us
    all_gather x1, blocking collectives, on_device(): gathered = lax.all_gather(pix_factor, 'peak', axis=0, tiled=True)  20.3 us
    dot_general x8, matrix products, on_device(): lax.dot_general(cube[:, index, :], gathered, (((0,), (0,)), ((), ())), pr...  12.3 us
    dot_general x1, matrix products, on_device(): jnp.dot(cube.reshape(pixels * sections, peaks), peak_factor, preferred_el...  7.95 us
    unnamed x7, local copies, waits for them, and re-layouts  7.71 us
  transfers between devices with their start and end apart: 1, of which 0 were waited for; matrix products, arithmetic and copies ran while one was open for 8% of the time, Pallas kernels for 0%

commit v1 on v0

v1 whole, which is shorter than its diff:
```python
import math

import jax
import jax.numpy as jnp
from jax import lax
from jax.experimental import pallas as pl
from jax.experimental.pallas import tpu as pltpu
from jax.sharding import Mesh
from jax.sharding import PartitionSpec as P

f32, bf16 = jnp.float32, jnp.bfloat16
NN = (((1,), (0,)), ((), ()))
NT = (((1,), (1,)), ((), ()))
PIX = ("xh", "z")
PEAK = ("y", "xl", "c")


def dot(a, b, dims=NN):
    return lax.dot_general(a, b, dims, preferred_element_type=f32)


def dot_split(w, b, dims=NN):
    hi = w.astype(bf16)
    rest = w - hi.astype(f32)
    mid = rest.astype(bf16)
    low = (rest - mid.astype(f32)).astype(bf16)
    return dot(hi, b, dims) + (dot(mid, b, dims) + dot(low, b, dims))


def both_modes(core, cube, own, other, ct_ref, b_ref, keep, send, peak, xbuf, wide, flat, wt, acc, sems):
    blocks, sections = xbuf.shape[0], b_ref.shape[0]
    pixels = xbuf.shape[1] // sections
    rank, peaks = ct_ref.shape
    mine = core[0]

    def copy(step):
        index = 2 * (step // 2) + lax.bitwise_xor(mine, step % 2)
        return pltpu.make_async_copy(cube.at[index], xbuf.at[step], sems.at[step])

    for step in range(blocks):
        copy(step).start()
    bt = jnp.transpose(b_ref[...].astype(f32))
    ct = ct_ref[...]
    for s in range(sections):
        product = ct.astype(f32) * bt[:, s : s + 1]
        hi = product.astype(bf16)
        wt[0:rank, s * peaks : (s + 1) * peaks] = hi
        wt[rank:, s * peaks : (s + 1) * peaks] = (product - hi.astype(f32)).astype(bf16)
    gram_b = dot(bt.astype(bf16), bt.astype(bf16), NT)
    weight = gram_b * dot(ct, ct, NT)
    gram_a = jnp.zeros((rank, rank), f32)
    acc[...] = jnp.zeros_like(acc)
    for step in range(blocks):
        at = own[step // 2] if step % 2 == 0 else other[step // 2]
        slot = step % 2
        gram_a = gram_a + dot(at, at, NT)
        copy(step).wait()
        wide[slot] = xbuf[step].astype(f32)
        for s in range(sections):
            rows = wide[slot, pl.ds(s, pixels, stride=sections), :]
            flat[slot, :, s * peaks : (s + 1) * peaks] = rows.astype(bf16)
        y = flat[slot]
        out = dot(wt[...], y, NT)
        out = out[0:rank] + out[rank:] - dot_split(weight, at)
        if step % 2 == 0:
            keep[step // 2] = out
        else:
            send[step // 2] = out
        acc[...] += dot(at, y)
    total = -dot_split(gram_a * gram_b, ct)
    for s in range(sections):
        total = total + acc[:, s * peaks : (s + 1) * peaks] * bt[:, s : s + 1]
    peak[...] = total


def call_both_modes(core, cube, own, other, ct, b):
    blocks, rows, peaks = cube.shape
    half, rank, pixels = own.shape
    vmem = pl.BlockSpec(memory_space=pltpu.VMEM)
    return pl.pallas_call(
        both_modes,
        out_shape=(
            jax.ShapeDtypeStruct((half, rank, pixels), f32),
            jax.ShapeDtypeStruct((half, rank, pixels), f32),
            jax.ShapeDtypeStruct((rank, peaks), f32),
        ),
        in_specs=[pl.BlockSpec(memory_space=pltpu.SMEM), pl.BlockSpec(memory_space=pltpu.HBM)] + [vmem] * 4,
        out_specs=(vmem, vmem, vmem),
        scratch_shapes=[
            pltpu.VMEM((blocks, rows, peaks), bf16),
            pltpu.VMEM((2, rows, peaks), f32),
            pltpu.VMEM((2, pixels, rows // pixels * peaks), bf16),
            pltpu.VMEM((2 * rank, rows // pixels * peaks), bf16),
            pltpu.VMEM((rank, rows // pixels * peaks), f32),
            pltpu.SemaphoreType.DMA((blocks,)),
        ],
        compiler_params=pltpu.CompilerParams(vmem_limit_bytes=40 << 20),
        cost_estimate=pl.CostEstimate(flops=3 * 10**9, bytes_accessed=10 << 20, transcendentals=0),
        name="both_modes",
    )(core, cube, own, other, ct, b)


def on_device(cube, pix_factor, sec_factor, peak_factor):
    pixels, sections, peaks = cube.shape
    rank = peak_factor.shape[1]
    core = lax.axis_index("c").astype(jnp.int32).reshape(1)
    swap = [(0, 1), (1, 0)]
    at = pix_factor.T
    ct = peak_factor.T
    own_pixels = at.shape[1]
    spread = jnp.broadcast_to(at[None], (8,) + at.shape)
    own = lax.all_to_all(spread, ("y", "xl"), 0, 0, tiled=True)
    other = lax.ppermute(own, "c", swap)
    cube = cube.reshape(pixels // own_pixels, own_pixels * sections, peaks)
    keep, send, part = call_both_modes(core, cube, own, other, ct, sec_factor)
    keep = keep + lax.ppermute(send, "c", swap)
    blocks = lax.all_to_all(keep, ("y", "xl"), 0, 0, tiled=True)
    grad_pix = jnp.sum(blocks, axis=0).T
    copies = jnp.broadcast_to(part[None], (16,) + part.shape)
    parts = lax.all_to_all(copies, PIX, 0, 0, tiled=True)
    scale = 1.0 / math.sqrt(float(sections * pixels * 16))
    grad_peak = (jnp.sum(parts, axis=0) * scale).T
    return (grad_pix, grad_peak)


def solution(mesh):
    split = Mesh(mesh.devices.reshape(2, 8, 4, 2, 2), PIX + PEAK)
    in_specs = (P(PIX, None, PEAK), P(PIX + PEAK, None), P(), P(PEAK, None))
    out_specs = (P(PIX + PEAK, None), P(PEAK, None))
    return jax.shard_map(
        on_device, mesh=split, in_specs=in_specs, out_specs=out_specs, check_vma=False
    )
```

time: 274 us -> 71.8 us (0.26); the launches traced: 270 us -> 71.3 us
  blocking collectives: 224 us -> 11.8 us
  waiting for transfers between devices: 0.02 us -> 24.7 us
  matrix products: 23.3 us -> 0 us
  starting transfers between devices: 0.04 us -> 15.4 us
  between operations: 14.1 us -> 0.67 us
  Pallas kernels: 0 us -> 10.1 us
    psum x3 -> x0, blocking collectives: 204 us -> none  [the longest x1 78.9 us: on_device(): gram_a = lax.psum(local_a, ('pix', 'peak'))]
    dot_general x14 -> x0, matrix products: 23.3 us -> none  [the longest x8 12.3 us: on_device(): lax.dot_general(cube[:, index, :], gathered, (((0,), (0,)), ((), ())), pr...]
    all_to_all x0 -> x2, waiting for transfers between devices: none -> 21.3 us  [the longest x1 14.4 us: on_device(): parts = lax.all_to_all(copies, PIX, 0, 0, tiled=True)]
    all_gather x1 -> x0, blocking collectives: 20.3 us -> none  [on_device(): gathered = lax.all_gather(pix_factor, 'peak', axis=0, tiled=True)]
    all_to_all x0 -> x2, starting transfers between devices: none -> 15.3 us  [the longest x1 10.1 us: on_device(): parts = lax.all_to_all(copies, PIX, 0, 0, tiled=True)]
    all_to_all x0 -> x1, blocking collectives: none -> 11.8 us  [on_device(): own = lax.all_to_all(spread, ('y', 'xl'), 0, 0, tiled=True)]
    pallas_call x0 -> x1, Pallas kernels: none -> 10.1 us  [call_both_modes(): pl.pallas_call(both_modes, out_shape=(jax.ShapeDtypeStruct((half, rank, p...]
    ppermute x0 -> x2, waiting for transfers between devices: none -> 3.43 us  [the longest x1 1.9 us: on_device(): keep = keep + lax.ppermute(send, 'c', swap)]
  transfers between devices with their start and end apart: 1 -> 4, of which waited for: 0 -> 4; matrix products, arithmetic and copies ran while one was open for 8% -> 2% of each run, Pallas kernels for 0% -> 0%
where the time goes in v1:
time: 71.8 us; the launch traced here: 71.3 us
  waiting for transfers between devices  24.7 us (34%)
  starting transfers between devices  15.4 us (21%)
  blocking collectives  11.8 us (16%)
  Pallas kernels  10.1 us (14%)
  local copies, waits for them, and re-layouts  6.4 us (9%)
  other arithmetic  2.19 us (3%)
    all_to_all x1, waiting for transfers between devices, on_device(): parts = lax.all_to_all(copies, PIX, 0, 0, tiled=True)  14.4 us
    all_to_all x1, blocking collectives, on_device(): own = lax.all_to_all(spread, ('y', 'xl'), 0, 0, tiled=True)  11.8 us
    all_to_all x1, starting transfers between devices, on_device(): parts = lax.all_to_all(copies, PIX, 0, 0, tiled=True)  10.1 us
    pallas_call x1, Pallas kernels, call_both_modes(): pl.pallas_call(both_modes, out_shape=(jax.ShapeDtypeStruct((half, rank, p...  10.1 us
    all_to_all x1, waiting for transfers between devices, on_device(): blocks = lax.all_to_all(keep, ('y', 'xl'), 0, 0, tiled=True)  6.89 us
    all_to_all x1, starting transfers between devices, on_device(): blocks = lax.all_to_all(keep, ('y', 'xl'), 0, 0, tiled=True)  5.17 us
    unnamed x6, local copies, waits for them, and re-layouts  4.78 us
    ppermute x1, waiting for transfers between devices, on_device(): keep = keep + lax.ppermute(send, 'c', swap)  1.9 us
  transfers between devices with their start and end apart: 4, of which 4 were waited for; matrix products, arithmetic and copies ran while one was open for 2% of the time, Pallas kernels for 0%

profile of v1, /device:TPU:2, one launch (start us, length us, event | category | flops | bytes accessed | tf_op | source)
XLA Modules:
  0.0 71.3 jit_solution(4020216294763979573)
XLA Ops:
  0.6 0.8 %broadcast_in_dim.4 = bf16[8,64,256]{2,1,0:T(8,128)(2,1)S(1)} broadcast(bf16[64,256]{1,0:T(8,128)(2,1)} %bitcast.10), dimensions={1,2} | broadcast | bytes 294912 | tf_op jit(solution)/shard_map/broadcast_in_dim | solution.py:111
  1.4 11.8 %all_to_all.15.own = bf16[8,64,256]{2,1,0:T(8,128)(2,1)S(1)} all-to-all(bf16[8,64,256]{2,1,0:T(8,128)(2,1)S(1)} %broadcast_in_dim.4), channel_id=1, replica_groups=mesh['xh'=2,'z'=8,'y'=4,'xl'=2,'c'=2] {'y','xl'}, dimensions={0} | all-to-all | bytes 524288 | tf_op jit(solution)/shard_map/all_to_all | solution.py:112
  13.3 0.0 collective-permute-start
  13.3 1.5 %collective-permute-done.other = bf16[8,64,256]{2,1,0:T(8,128)(2,1)S(1)} collective-permute-done((bf16[8,64,256]{2,1,0:T(8,128)(2,1)S(1)}, bf16[8,64,256]{2,1,0:T(8,128)(2,1)S(1)}, u32[]{:S(2)}, u32[]{:S(2)}) %collective-permute-start) | collective-permute-done | bytes 262176 | tf_op jit(solution)/shard_map/ppermute | solution.py:113
  14.8 0.0 copy-start
  14.8 3.4 %copy-done = bf16[4096,8,128]{2,1,0:T(8,128)(2,1)S(1)} copy-done((bf16[4096,8,128]{2,1,0:T(8,128)(2,1)S(1)}, bf16[4096,8,128]{2,1,0:T(8,128)(2,1)}, u32[]{:S(2)}) %copy-start) | copy-done | bytes 8388632
  18.2 0.0 copy-start.1
  18.2 0.7 %copy-done.1 = bf16[128,64]{0,1:T(8,128)(2,1)S(1)} copy-done((bf16[128,64]{0,1:T(8,128)(2,1)S(1)}, bf16[128,64]{0,1:T(8,128)(2,1)}, u32[]{:S(2)}) %copy-start.1) | copy-done | bytes 16408
  18.9 0.0 copy-start.2
  18.9 0.7 copy-done.2
  19.6 10.1 %both_modes.1 = (f32[8,64,256]{2,1,0:T(8,128)S(1)}, f32[8,64,256]{2,1,0:T(8,128)S(1)}, f32[64,128]{1,0:T(8,128)S(1)}) custom-call(s32[1]{0:T(128)} %bitcast.core, bf16[16,2048,128]{2,1,0:T(8,128)(2,1)S(1)} %bitcast.7, bf16[8,64,256]{2,1,0:T(8,128)(2,1)S(1)} %all_to_all.15.own, bf16[8,64,256]{2,1,0:T(8,128)(2,1)S(1)} %collective-permute-done.other, ...), custom_call_target="tpu_custom_call" | custom-call | flops 3000000000 | bytes 10485760 | tf_op jit(solution)/shard_map/both_modes/pallas_call | solution.py:80
  29.7 0.8 %broadcast_in_dim.5 = f32[16,64,128]{2,1,0:T(8,128)} broadcast(f32[64,128]{1,0:T(8,128)S(1)} %get-tuple-element.7), dimensions={1,2} | broadcast | bytes 557056 | tf_op jit(solution)/shard_map/broadcast_in_dim | solution.py:119
  30.5 10.1 %all-to-all-start.2 = ((f32[16,64,128]{2,1,0:T(8,128)}), f32[16,64,128]{2,1,0:T(8,128)S(1)}, u32[]{:S(2)}, u32[]{:S(2)}) async-start(f32[16,64,128]{2,1,0:T(8,128)} %broadcast_in_dim.5), calls=%async_computation.2 | async-start | bytes 1048576 | tf_op jit(solution)/shard_map/all_to_all | solution.py:120
  40.7 0.1 collective-permute-start.1
  40.8 1.9 %collective-permute-done.1 = f32[8,64,256]{2,1,0:T(8,128)S(1)} collective-permute-done((f32[8,64,256]{2,1,0:T(8,128)S(1)}, f32[8,64,256]{2,1,0:T(8,128)S(1)}, u32[]{:S(2)}, u32[]{:S(2)}) %collective-permute-start.1) | collective-permute-done | bytes 524320 | tf_op jit(solution)/shard_map/ppermute | solution.py:116
  42.7 0.9 %add.3 = f32[8,64,256]{2,1,0:T(8,128)} add(f32[8,64,256]{2,1,0:T(8,128)S(1)} %get-tuple-element.5, f32[8,64,256]{2,1,0:T(8,128)S(1)} %collective-permute-done.1) | non-fusion elementwise | flops 131072 | bytes 1572864 | tf_op jit(solution)/shard_map/add | solution.py:116
  43.5 14.4 %all-to-all-done.2 = f32[16,64,128]{2,1,0:T(8,128)S(1)} async-done(((f32[16,64,128]{2,1,0:T(8,128)}), f32[16,64,128]{2,1,0:T(8,128)S(1)}, u32[]{:S(2)}, u32[]{:S(2)}) %all-to-all-start.2) | async-done | bytes 524320 | tf_op jit(solution)/shard_map/all_to_all | solution.py:120
  57.9 5.2 %all-to-all-start.1 = ((f32[8,64,256]{2,1,0:T(8,128)}), f32[8,64,256]{2,1,0:T(8,128)S(1)}, u32[]{:S(2)}, u32[]{:S(2)}) async-start(f32[8,64,256]{2,1,0:T(8,128)} %add.3), calls=%async_computation.1 | async-start | bytes 1048576 | tf_op jit(solution)/shard_map/all_to_all | solution.py:117
  63.1 0.6 multiply_bitcast_fusion
  63.7 6.9 %all-to-all-done.1 = f32[8,64,256]{2,1,0:T(8,128)S(1)} async-done(((f32[8,64,256]{2,1,0:T(8,128)}), f32[8,64,256]{2,1,0:T(8,128)S(1)}, u32[]{:S(2)}, u32[]{:S(2)}) %all-to-all-start.1) | async-done | bytes 524320 | tf_op jit(solution)/shard_map/all_to_all | solution.py:117
  70.6 0.7 reduce_sum.18
  (1 shorter events, 0.0 us)
Async XLA Ops:
  13.3 1.5 %collective-permute-start = (bf16[8,64,256]{2,1,0:T(8,128)(2,1)S(1)}, bf16[8,64,256]{2,1,0:T(8,128)(2,1)S(1)}, u32[]{:S(2)}, u32[]{:S(2)}) collective-permute-start(bf16[8,64,256]{2,1,0:T(8,128)(2,1)S(1)} %all_to_all.15.own), channel_id=1, source_target_pairs={{0,1},{1,0},{2,3},{3,2},{4,5},{5,4},{6,7},{7,6},{8,9},{9,8},{10,11... | collective-permute-start | bytes 786440 | tf_op jit(solution)/shard_map/ppermute | solution.py:113
  14.8 3.4 %copy-start = (bf16[4096,8,128]{2,1,0:T(8,128)(2,1)S(1)}, bf16[4096,8,128]{2,1,0:T(8,128)(2,1)}, u32[]{:S(2)}) copy-start(bf16[4096,8,128]{2,1,0:T(8,128)(2,1)} %param.4) | copy-start | bytes 25165828
  18.2 0.7 %copy-start.1 = (bf16[128,64]{0,1:T(8,128)(2,1)S(1)}, bf16[128,64]{0,1:T(8,128)(2,1)}, u32[]{:S(2)}) copy-start(bf16[128,64]{0,1:T(8,128)(2,1)} %param.7) | copy-start | bytes 49156
  18.9 0.7 copy-start.2
  30.5 27.4 %all-to-all-start.2 = ((f32[16,64,128]{2,1,0:T(8,128)}), f32[16,64,128]{2,1,0:T(8,128)S(1)}, u32[]{:S(2)}, u32[]{:S(2)}) async-start(f32[16,64,128]{2,1,0:T(8,128)} %broadcast_in_dim.5), calls=%async_computation.2 | async-start | bytes 1048576 | tf_op jit(solution)/shard_map/all_to_all | solution.py:120
  40.7 2.0 %collective-permute-start.1 = (f32[8,64,256]{2,1,0:T(8,128)S(1)}, f32[8,64,256]{2,1,0:T(8,128)S(1)}, u32[]{:S(2)}, u32[]{:S(2)}) collective-permute-start(f32[8,64,256]{2,1,0:T(8,128)S(1)} %get-tuple-element.6), channel_id=1, source_target_pairs={{0,1},{1,0},{2,3},{3,2},{4,5},{5,4},{6,7},{7,6},{8,9},{9,8},{10,11... | collective-permute-start | bytes 1572872 | tf_op jit(solution)/shard_map/ppermute | solution.py:116
  57.9 12.7 %all-to-all-start.1 = ((f32[8,64,256]{2,1,0:T(8,128)}), f32[8,64,256]{2,1,0:T(8,128)S(1)}, u32[]{:S(2)}, u32[]{:S(2)}) async-start(f32[8,64,256]{2,1,0:T(8,128)} %add.3), calls=%async_computation.1 | async-start | bytes 1048576 | tf_op jit(solution)/shard_map/all_to_all | solution.py:117

commit v2 on v1

v2 whole, which is shorter than its diff:
```python
import math

import jax
import jax.numpy as jnp
from jax import lax
from jax.experimental import pallas as pl
from jax.experimental.pallas import tpu as pltpu
from jax.sharding import Mesh
from jax.sharding import PartitionSpec as P

f32, bf16 = jnp.float32, jnp.bfloat16
NN = (((1,), (0,)), ((), ()))
NT = (((1,), (1,)), ((), ()))
PIX = ("xh", "z")
PEAK = ("y", "xl", "c")
VMEM = pl.BlockSpec(memory_space=pltpu.VMEM)
ANY = pl.BlockSpec(memory_space=pl.ANY)
GRANT = 56 << 20


def dot(a, b, dims=NN):
    return lax.dot_general(a, b, dims, preferred_element_type=f32)


def dot_split(w, b, dims=NN):
    hi = w.astype(bf16)
    rest = w - hi.astype(f32)
    mid = rest.astype(bf16)
    low = (rest - mid.astype(f32)).astype(bf16)
    return dot(hi, b, dims) + (dot(mid, b, dims) + dot(low, b, dims))


def by_pixel(source, wide, sections):
    pixels = source.shape[0] // sections
    wide[...] = source[...].astype(f32)
    return jnp.concatenate(
        [wide[pl.ds(s, pixels, stride=sections), :].astype(bf16) for s in range(sections)], axis=1
    )


def stream(cube, xbuf, sems, ahead, body):
    pairs = xbuf.shape[0]

    def copy(pair):
        return pltpu.make_async_copy(cube.at[pl.ds(2 * pair, 2)], xbuf.at[pair], sems.at[pair])

    for pair in range(ahead):
        copy(pair).start()
    yield
    for pair in range(pairs):
        if pair + ahead < pairs:
            copy(pair + ahead).start()
        copy(pair).wait()
        body(pair)
    yield


def pixel_mode(cube, ct_hbm, b_hbm, out, ct_ref, b_ref, xbuf, wide, wt, obuf, insems, sems, outsems):
    sections = b_ref.shape[0]
    rank, peaks = ct_ref.shape
    small = [
        pltpu.make_async_copy(ct_hbm, ct_ref, insems.at[0]),
        pltpu.make_async_copy(b_hbm, b_ref, insems.at[1]),
    ]
    for each in small:
        each.start()

    def copy_out(pair):
        two = pl.ds(2 * pair, 2)
        return pltpu.make_async_copy(obuf.at[two], out.at[two], outsems.at[pair])

    def body(pair):
        for part in range(2):
            y = by_pixel(xbuf.at[pair, part], wide.at[part], sections)
            both = jnp.transpose(dot(y, wt[...]))
            obuf[2 * pair + part, 0:rank] = both[0:rank] + both[rank:]
            obuf[2 * pair + part, rank:] = gram
        copy_out(pair).start()

    run = stream(cube, xbuf, sems, 2, body)
    next(run)
    for each in small:
        each.wait()
    bt = jnp.transpose(b_ref[...].astype(f32))
    ct = ct_ref[...]
    gram = dot(ct, ct, NT)
    quarter = rank // 4
    gram = jnp.concatenate([gram[i * quarter : (i + 1) * quarter] for i in range(4)], axis=1)
    for s in range(sections):
        product = ct.astype(f32) * bt[:, s : s + 1]
        hi = product.astype(bf16).astype(f32)
        both = jnp.concatenate([hi, product - hi], axis=0)
        wt[s * peaks : (s + 1) * peaks, :] = jnp.transpose(both).astype(bf16)
    next(run)
    for pair in range(xbuf.shape[0]):
        copy_out(pair).wait()


def call_pixel_mode(cube, ct, b):
    blocks, rows, peaks = cube.shape
    rank = ct.shape[0]
    sections = b.shape[0]
    part = (blocks, rank + rank // 4, rows // sections)
    return pl.pallas_call(
        pixel_mode,
        out_shape=jax.ShapeDtypeStruct(part, f32),
        in_specs=[ANY, ANY, ANY],
        out_specs=ANY,
        scratch_shapes=[
            pltpu.VMEM(ct.shape, bf16),
            pltpu.VMEM(b.shape, bf16),
            pltpu.VMEM((blocks // 2, 2, rows, peaks), bf16),
            pltpu.VMEM((2, rows, peaks), f32),
            pltpu.VMEM((sections * peaks, 2 * rank), bf16),
            pltpu.VMEM(part, f32),
            pltpu.SemaphoreType.DMA((2,)),
            pltpu.SemaphoreType.DMA((blocks // 2,)),
            pltpu.SemaphoreType.DMA((blocks // 2,)),
        ],
        compiler_params=pltpu.CompilerParams(vmem_limit_bytes=GRANT),
        cost_estimate=pl.CostEstimate(flops=2 * 10**9, bytes_accessed=20 << 20, transcendentals=0),
        name="pixel_mode",
    )(cube, ct, b)


def peak_mode(cube, rows_hbm, ct_hbm, b_hbm, peak, rows, ct_ref, b_ref, xbuf, wide, acc, insems, sems):
    sections, rank = b_ref.shape
    peaks = peak.shape[1]
    small = [
        pltpu.make_async_copy(rows_hbm, rows, insems.at[0]),
        pltpu.make_async_copy(ct_hbm, ct_ref, insems.at[1]),
        pltpu.make_async_copy(b_hbm, b_ref, insems.at[2]),
    ]
    for each in small:
        each.start()

    def body(pair):
        total = None
        for part in range(2):
            y = by_pixel(xbuf.at[pair, part], wide.at[2 * (pair % 2) + part], sections)
            term = dot(rows[2 * pair + part], y)
            total = term if total is None else total + term
        acc[...] += total

    run = stream(cube, xbuf, sems, 3, body)
    next(run)
    for each in small:
        each.wait()
    bt = jnp.transpose(b_ref[...].astype(f32))
    gram_a = jnp.zeros((rank, rank), f32)
    for index in range(rows.shape[0]):
        gram_a = gram_a + dot(rows[index], rows[index], NT)
    gram_b = dot(bt.astype(bf16), bt.astype(bf16), NT)
    total = -dot_split(gram_a * gram_b, ct_ref[...])
    acc[...] = jnp.zeros_like(acc)
    next(run)
    for s in range(sections):
        total = total + acc[:, s * peaks : (s + 1) * peaks] * bt[:, s : s + 1]
    peak[...] = total


def call_peak_mode(cube, own, ct, b):
    blocks, rows, peaks = cube.shape
    rank = ct.shape[0]
    return pl.pallas_call(
        peak_mode,
        out_shape=jax.ShapeDtypeStruct((rank, peaks), f32),
        in_specs=[ANY, ANY, ANY, ANY],
        out_specs=VMEM,
        scratch_shapes=[
            pltpu.VMEM(own.shape, bf16),
            pltpu.VMEM(ct.shape, bf16),
            pltpu.VMEM(b.shape, bf16),
            pltpu.VMEM((blocks // 2, 2, rows, peaks), bf16),
            pltpu.VMEM((4, rows, peaks), f32),
            pltpu.VMEM((rank, b.shape[0] * peaks), f32),
            pltpu.SemaphoreType.DMA((3,)),
            pltpu.SemaphoreType.DMA((blocks // 2,)),
        ],
        compiler_params=pltpu.CompilerParams(vmem_limit_bytes=GRANT),
        cost_estimate=pl.CostEstimate(flops=10**9, bytes_accessed=10 << 20, transcendentals=0),
        name="peak_mode",
    )(cube, own, ct, b)


def finish_pixels(blocks, at_ref, b_ref, out):
    rank = out.shape[0]
    total = blocks[0]
    for index in range(1, blocks.shape[0]):
        total = total + blocks[index]
    gram = total[rank:]
    gram_c = jnp.concatenate([gram[:, i * rank : (i + 1) * rank] for i in range(4)], axis=0)
    bt = jnp.transpose(b_ref[...].astype(f32)).astype(bf16)
    out[...] = total[0:rank] - dot_split(dot(bt, bt, NT) * gram_c, at_ref[...])


def call_finish_pixels(blocks, at, b):
    return pl.pallas_call(
        finish_pixels,
        out_shape=jax.ShapeDtypeStruct(at.shape, f32),
        in_specs=[VMEM] * 3,
        out_specs=VMEM,
        cost_estimate=pl.CostEstimate(flops=10**7, bytes_accessed=1 << 20, transcendentals=0),
        name="finish_pixels",
    )(blocks, at, b)


def on_device(cube, pix_factor, sec_factor, peak_factor):
    pixels, sections, peaks = cube.shape
    at = pix_factor.T
    ct = peak_factor.T
    cube = cube.reshape(pixels // at.shape[1], at.shape[1] * sections, peaks)
    own = lax.all_to_all(jnp.broadcast_to(at[None], (16,) + at.shape), PEAK, 0, 0, tiled=True)
    sums = call_pixel_mode(cube, ct, sec_factor)
    sums, own = lax.optimization_barrier((sums, own))
    part = call_peak_mode(cube, own, ct, sec_factor)
    sums, part = lax.optimization_barrier((sums, part))
    blocks = lax.all_to_all(sums, PEAK, 0, 0, tiled=True)
    for axis, step in (("z", 1), ("z", 2), ("z", 4)):
        pairs = [(i, i ^ step) for i in range(lax.axis_size(axis))]
        part = part + lax.ppermute(part, axis, pairs)
    other = lax.ppermute(part, "xh", [(0, 1), (1, 0)])
    grad_pix = call_finish_pixels(blocks, at, sec_factor).T
    other, grad_pix = lax.optimization_barrier((other, grad_pix))
    part = part + other
    scale = 1.0 / math.sqrt(float(sections * pixels * 16))
    grad_peak = (part * scale).T
    return (grad_pix, grad_peak)


def solution(mesh):
    split = Mesh(mesh.devices.reshape(2, 8, 4, 2, 2), PIX + PEAK)
    in_specs = (P(PIX, None, PEAK), P(PIX + PEAK, None), P(), P(PEAK, None))
    out_specs = (P(PIX + PEAK, None), P(PEAK, None))
    return jax.shard_map(
        on_device, mesh=split, in_specs=in_specs, out_specs=out_specs, check_vma=False
    )
```

time: 71.8 us -> 55 us (0.77)
  waiting for transfers between devices: 24.7 us -> 7.74 us
  blocking collectives: 11.8 us -> 0 us
  starting transfers between devices: 15.4 us -> 24.9 us
  Pallas kernels: 10.1 us -> 16.5 us
  local copies, waits for them, and re-layouts: 6.4 us -> 3.55 us
  other arithmetic: 2.19 us -> 0.64 us
    all_to_all x2, waiting for transfers between devices: 21.3 us -> 1.94 us  [the longest x1 1.94 us: on_device(): lax.all_to_all(jnp.broadcast_to(at[None], (16,) + at.shape), PEAK, 0, 0,...]
    ppermute x2 -> x4, starting transfers between devices: 0.1 us -> 14.2 us  [the longest x3 12.1 us: on_device(): part = part + lax.ppermute(part, axis, pairs)]
    all_to_all x1 -> x0, blocking collectives: 11.8 us -> none  [on_device(): own = lax.all_to_all(spread, ('y', 'xl'), 0, 0, tiled=True)]
    pallas_call x1 -> x3, Pallas kernels: 10.1 us -> 16.5 us  [the longest x1 7.79 us: call_pixel_mode(): pl.pallas_call(pixel_mode, out_shape=jax.ShapeDtypeStruct(part, f32), in_...]
    all_to_all x2, starting transfers between devices: 15.3 us -> 10.7 us  [the longest x1 5.94 us: on_device(): lax.all_to_all(jnp.broadcast_to(at[None], (16,) + at.shape), PEAK, 0, 0,...]
    unnamed x6, local copies, waits for them, and re-layouts: 4.78 us -> 1.92 us
    ppermute x2 -> x4, waiting for transfers between devices: 3.43 us -> 5.8 us  [the longest x3 5.8 us: on_device(): part = part + lax.ppermute(part, axis, pairs)]
    add x1 -> x3, other arithmetic: 0.87 us -> 0.02 us  [on_device(): part = part + lax.ppermute(part, axis, pairs)]
  transfers between devices with their start and end apart: 4 -> 6, of which waited for: 4 -> 4; matrix products, arithmetic and copies ran while one was open for 2% -> 0% of each run, Pallas kernels for 0% -> 19%
where the time goes in v2:
time: 55 us; the launch traced here: 54 us
  starting transfers between devices  24.9 us (45%)
  Pallas kernels  16.5 us (30%)
  waiting for transfers between devices  7.74 us (14%)
  local copies, waits for them, and re-layouts  3.55 us (6%)
  between operations  0.67 us (1%)
  other arithmetic  0.64 us (1%)
    ppermute x3, starting transfers between devices, on_device(): part = part + lax.ppermute(part, axis, pairs)  12.1 us
    pallas_call x1, Pallas kernels, call_pixel_mode(): pl.pallas_call(pixel_mode, out_shape=jax.ShapeDtypeStruct(part, f32), in_...  7.79 us
    pallas_call x1, Pallas kernels, call_peak_mode(): pl.pallas_call(peak_mode, out_shape=jax.ShapeDtypeStruct((rank, peaks), f...  6.39 us
    all_to_all x1, starting transfers between devices, on_device(): lax.all_to_all(jnp.broadcast_to(at[None], (16,) + at.shape), PEAK, 0, 0,...  5.94 us
    ppermute x3, waiting for transfers between devices, on_device(): part = part + lax.ppermute(part, axis, pairs)  5.8 us
    all_to_all x1, starting transfers between devices, on_device(): blocks = lax.all_to_all(sums, PEAK, 0, 0, tiled=True)  4.73 us
    pallas_call x1, Pallas kernels, call_finish_pixels(): pl.pallas_call(finish_pixels, out_shape=jax.ShapeDtypeStruct(at.shape, f3...  2.33 us
    ppermute x1, starting transfers between devices, on_device(): other = lax.ppermute(part, 'xh', [(0, 1), (1, 0)])  2.12 us
  transfers between devices with their start and end apart: 6, of which 4 were waited for; matrix products, arithmetic and copies ran while one was open for 0% of the time, Pallas kernels for 19%

profile of v2, /device:TPU:2, one launch (start us, length us, event | category | flops | bytes accessed | tf_op | source)
XLA Modules:
  0.0 54.0 jit_solution(4118915123942260385)
XLA Ops:
  0.6 1.6 %broadcast_in_dim.2 = bf16[16,64,256]{2,1,0:T(8,128)(2,1)} broadcast(bf16[64,256]{1,0:T(8,128)(2,1)} %bitcast.8), dimensions={1,2} | broadcast | bytes 557056 | tf_op jit(solution)/shard_map/broadcast_in_dim | solution.py:213
  2.3 5.9 %all-to-all-start = ((bf16[16,64,256]{2,1,0:T(8,128)(2,1)}), bf16[16,64,256]{2,1,0:T(8,128)(2,1)S(1)}, u32[]{:S(2)}, u32[]{:S(2)}) async-start(bf16[16,64,256]{2,1,0:T(8,128)(2,1)} %broadcast_in_dim.2), calls=%async_computation | async-start | bytes 1048576 | tf_op jit(solution)/shard_map/all_to_all | solution.py:213
  8.2 7.8 %pixel_mode.1 = f32[16,80,256]{2,1,0:T(8,128)} custom-call(bf16[16,2048,128]{2,1,0:T(8,128)(2,1)} %bitcast.6, bf16[64,128]{1,0:T(8,128)(2,1)} %bitcast.10, bf16[8,64]{1,0:T(8,128)(2,1)} %b_ref.1), custom_call_target="tpu_custom_call" | custom-call | flops 2000000000 | bytes 20971520 | tf_op jit(solution)/shard_map/pixel_mode/pallas_call | solution.py:104
  16.0 1.9 %all-to-all-done.rows_hbm = bf16[16,64,256]{2,1,0:T(8,128)(2,1)S(1)} async-done(((bf16[16,64,256]{2,1,0:T(8,128)(2,1)}), bf16[16,64,256]{2,1,0:T(8,128)(2,1)S(1)}, u32[]{:S(2)}, u32[]{:S(2)}) %all-to-all-start) | async-done | bytes 524320 | tf_op jit(solution)/shard_map/all_to_all | solution.py:213
  17.9 0.0 copy-start.1
  17.9 0.8 %copy-done.1 = bf16[16,64,256]{2,1,0:T(8,128)(2,1)} copy-done((bf16[16,64,256]{2,1,0:T(8,128)(2,1)}, bf16[16,64,256]{2,1,0:T(8,128)(2,1)S(1)}, u32[]{:S(2)}) %copy-start.1) | copy-done | bytes 524312
  18.8 6.4 %peak_mode.1 = f32[64,128]{1,0:T(8,128)} custom-call(bf16[16,2048,128]{2,1,0:T(8,128)(2,1)} %bitcast.7, bf16[16,64,256]{2,1,0:T(8,128)(2,1)} %copy-done.1, bf16[64,128]{1,0:T(8,128)(2,1)} %bitcast.11, bf16[8,64]{1,0:T(8,128)(2,1)} %b_ref.1), custom_call_target="tpu_custom_call" | custom-call | flops 1000000000 | bytes 10485760 | tf_op jit(solution)/shard_map/peak_mode/pallas_call | solution.py:165
  25.2 0.0 copy-start.2
  25.2 4.7 %all-to-all-start.1 = ((f32[16,80,256]{2,1,0:T(8,128)}), f32[16,80,256]{2,1,0:T(8,128)S(1)}, u32[]{:S(2)}, u32[]{:S(2)}) async-start(f32[16,80,256]{2,1,0:T(8,128)} %pixel_mode.1), calls=%async_computation.1 | async-start | bytes 2621440 | tf_op jit(solution)/shard_map/all_to_all | solution.py:218
  29.9 0.0 copy-done.2
  29.9 2.0 %collective-permute-start = (f32[64,128]{1,0:T(8,128)S(1)}, f32[64,128]{1,0:T(8,128)S(1)}, u32[]{:S(2)}, u32[]{:S(2)}) collective-permute-start(f32[64,128]{1,0:T(8,128)S(1)} %copy-done.2), channel_id=1, source_target_pairs={{0,16},{16,0},{32,48},{48,32},{64,80},{80,64},{96,112},{112,96},{1... | collective-permute-start | bytes 98312 | tf_op jit(solution)/shard_map/ppermute | solution.py:221
  31.9 2.0 %collective-permute-done = f32[64,128]{1,0:T(8,128)S(1)} collective-permute-done((f32[64,128]{1,0:T(8,128)S(1)}, f32[64,128]{1,0:T(8,128)S(1)}, u32[]{:S(2)}, u32[]{:S(2)}) %collective-permute-start) | collective-permute-done | bytes 32800 | tf_op jit(solution)/shard_map/ppermute | solution.py:221
  33.9 3.3 %collective-permute-start.1 = (f32[64,128]{1,0:T(8,128)S(1)}, f32[64,128]{1,0:T(8,128)S(1)}, u32[]{:S(2)}, u32[]{:S(2)}) collective-permute-start(f32[64,128]{1,0:T(8,128)S(1)} %add.12), channel_id=1, source_target_pairs={{0,32},{16,48},{32,0},{48,16},{64,96},{80,112},{96,64},{112,80},{1... | collective-permute-start | bytes 98312 | tf_op jit(solution)/shard_map/ppermute | solution.py:221
  37.2 1.9 %collective-permute-done.1 = f32[64,128]{1,0:T(8,128)S(1)} collective-permute-done((f32[64,128]{1,0:T(8,128)S(1)}, f32[64,128]{1,0:T(8,128)S(1)}, u32[]{:S(2)}, u32[]{:S(2)}) %collective-permute-start.1) | collective-permute-done | bytes 32800 | tf_op jit(solution)/shard_map/ppermute | solution.py:221
  39.1 6.8 %collective-permute-start.2 = (f32[64,128]{1,0:T(8,128)S(1)}, f32[64,128]{1,0:T(8,128)S(1)}, u32[]{:S(2)}, u32[]{:S(2)}) collective-permute-start(f32[64,128]{1,0:T(8,128)S(1)} %add.13), channel_id=1, source_target_pairs={{0,64},{16,80},{32,96},{48,112},{64,0},{80,16},{96,32},{112,48},{1... | collective-permute-start | bytes 98312 | tf_op jit(solution)/shard_map/ppermute | solution.py:221
  45.9 1.9 %collective-permute-done.2 = f32[64,128]{1,0:T(8,128)S(1)} collective-permute-done((f32[64,128]{1,0:T(8,128)S(1)}, f32[64,128]{1,0:T(8,128)S(1)}, u32[]{:S(2)}, u32[]{:S(2)}) %collective-permute-start.2) | collective-permute-done | bytes 32800 | tf_op jit(solution)/shard_map/ppermute | solution.py:221
  47.8 2.1 %collective-permute-start.3 = (f32[64,128]{1,0:T(8,128)S(1)}, f32[64,128]{1,0:T(8,128)S(1)}, u32[]{:S(2)}, u32[]{:S(2)}) collective-permute-start(f32[64,128]{1,0:T(8,128)S(1)} %add.14), channel_id=1, source_target_pairs={{0,128},{128,0},{1,129},{129,1},{2,130},{130,2},{3,131},{131,3},{4... | collective-permute-start | bytes 98312 | tf_op jit(solution)/shard_map/ppermute | solution.py:222
  50.0 0.0 all-to-all-done.1.blocks
  50.0 0.0 copy-start
  50.0 1.1 %copy-done = f32[16,80,256]{2,1,0:T(8,128)} copy-done((f32[16,80,256]{2,1,0:T(8,128)}, f32[16,80,256]{2,1,0:T(8,128)S(1)}, u32[]{:S(2)}) %copy-start) | copy-done | bytes 1310744
  51.1 2.3 %finish_pixels.1 = f32[64,256]{1,0:T(8,128)} custom-call(f32[16,80,256]{2,1,0:T(8,128)} %copy-done, bf16[64,256]{1,0:T(8,128)(2,1)} %bitcast.9, bf16[8,64]{1,0:T(8,128)(2,1)} %b_ref.1), custom_call_target="tpu_custom_call" | custom-call | flops 10000000 | bytes 1048576 | tf_op jit(solution)/shard_map/finish_pixels/pallas_call | solution.py:198
  53.4 0.0 collective-permute-done.3
  53.4 0.6 %multiply_bitcast_fusion = f32[128,64]{0,1:T(8,128)} fusion(f32[64,128]{1,0:T(8,128)S(1)} %add.14, f32[64,128]{1,0:T(8,128)S(1)} %collective-permute-done.3), kind=kLoop, calls=%fused_computation | loop fusion | flops 16384 | bytes 98304 | tf_op jit(solution)/shard_map/transpose | solution.py:227
  (3 shorter events, 0.0 us)
Async XLA Ops:
  2.3 15.7 %all-to-all-start = ((bf16[16,64,256]{2,1,0:T(8,128)(2,1)}), bf16[16,64,256]{2,1,0:T(8,128)(2,1)S(1)}, u32[]{:S(2)}, u32[]{:S(2)}) async-start(bf16[16,64,256]{2,1,0:T(8,128)(2,1)} %broadcast_in_dim.2), calls=%async_computation | async-start | bytes 1048576 | tf_op jit(solution)/shard_map/all_to_all | solution.py:213
  17.9 0.8 %copy-start.1 = (bf16[16,64,256]{2,1,0:T(8,128)(2,1)}, bf16[16,64,256]{2,1,0:T(8,128)(2,1)S(1)}, u32[]{:S(2)}) copy-start(bf16[16,64,256]{2,1,0:T(8,128)(2,1)S(1)} %all-to-all-done.rows_hbm) | copy-start | bytes 1572868
  25.2 4.7 %copy-start.2 = (f32[64,128]{1,0:T(8,128)S(1)}, f32[64,128]{1,0:T(8,128)}, u32[]{:S(2)}) copy-start(f32[64,128]{1,0:T(8,128)} %peak_mode.1) | copy-start | bytes 98308
  25.2 24.8 %all-to-all-start.1 = ((f32[16,80,256]{2,1,0:T(8,128)}), f32[16,80,256]{2,1,0:T(8,128)S(1)}, u32[]{:S(2)}, u32[]{:S(2)}) async-start(f32[16,80,256]{2,1,0:T(8,128)} %pixel_mode.1), calls=%async_computation.1 | async-start | bytes 2621440 | tf_op jit(solution)/shard_map/all_to_all | solution.py:218
  29.9 4.0 %collective-permute-start = (f32[64,128]{1,0:T(8,128)S(1)}, f32[64,128]{1,0:T(8,128)S(1)}, u32[]{:S(2)}, u32[]{:S(2)}) collective-permute-start(f32[64,128]{1,0:T(8,128)S(1)} %copy-done.2), channel_id=1, source_target_pairs={{0,16},{16,0},{32,48},{48,32},{64,80},{80,64},{96,112},{112,96},{1... | collective-permute-start | bytes 98312 | tf_op jit(solution)/shard_map/ppermute | solution.py:221
  33.9 5.2 %collective-permute-start.1 = (f32[64,128]{1,0:T(8,128)S(1)}, f32[64,128]{1,0:T(8,128)S(1)}, u32[]{:S(2)}, u32[]{:S(2)}) collective-permute-start(f32[64,128]{1,0:T(8,128)S(1)} %add.12), channel_id=1, source_target_pairs={{0,32},{16,48},{32,0},{48,16},{64,96},{80,112},{96,64},{112,80},{1... | collective-permute-start | bytes 98312 | tf_op jit(solution)/shard_map/ppermute | solution.py:221
  39.1 8.7 %collective-permute-start.2 = (f32[64,128]{1,0:T(8,128)S(1)}, f32[64,128]{1,0:T(8,128)S(1)}, u32[]{:S(2)}, u32[]{:S(2)}) collective-permute-start(f32[64,128]{1,0:T(8,128)S(1)} %add.13), channel_id=1, source_target_pairs={{0,64},{16,80},{32,96},{48,112},{64,0},{80,16},{96,32},{112,48},{1... | collective-permute-start | bytes 98312 | tf_op jit(solution)/shard_map/ppermute | solution.py:221
  47.8 5.6 %collective-permute-start.3 = (f32[64,128]{1,0:T(8,128)S(1)}, f32[64,128]{1,0:T(8,128)S(1)}, u32[]{:S(2)}, u32[]{:S(2)}) collective-permute-start(f32[64,128]{1,0:T(8,128)S(1)} %add.14), channel_id=1, source_target_pairs={{0,128},{128,0},{1,129},{129,1},{2,130},{130,2},{3,131},{131,3},{4... | collective-permute-start | bytes 98312 | tf_op jit(solution)/shard_map/ppermute | solution.py:222
  50.0 1.1 %copy-start = (f32[16,80,256]{2,1,0:T(8,128)}, f32[16,80,256]{2,1,0:T(8,128)S(1)}, u32[]{:S(2)}) copy-start(f32[16,80,256]{2,1,0:T(8,128)S(1)} %all-to-all-done.1.blocks) | copy-start | bytes 3932164

commit v3 on v2

--- a/solution.py
+++ b/solution.py
@@ -55,7 +55,7 @@
     yield
 
 
-def pixel_mode(cube, ct_hbm, b_hbm, out, ct_ref, b_ref, xbuf, wide, wt, obuf, insems, sems, outsems):
+def pixel_mode(core, cube, ct_hbm, b_hbm, keep, send, ct_ref, b_ref, xbuf, wide, wt, obuf, insems, sems, outsems):
     sections = b_ref.shape[0]
     rank, peaks = ct_ref.shape
     small = [
@@ -66,16 +66,19 @@
         each.start()
 
     def copy_out(pair):
-        two = pl.ds(2 * pair, 2)
-        return pltpu.make_async_copy(obuf.at[two], out.at[two], outsems.at[pair])
+        return [
+            pltpu.make_async_copy(obuf.at[part, pair], out.at[pair], outsems.at[part, pair])
+            for part, out in enumerate((keep, send))
+        ]
 
     def body(pair):
         for part in range(2):
-            y = by_pixel(xbuf.at[pair, part], wide.at[part], sections)
+            y = by_pixel(xbuf.at[pair, lax.bitwise_xor(core[0], part)], wide.at[part], sections)
             both = jnp.transpose(dot(y, wt[...]))
-            obuf[2 * pair + part, 0:rank] = both[0:rank] + both[rank:]
-            obuf[2 * pair + part, rank:] = gram
-        copy_out(pair).start()
+            obuf[part, pair, 0:rank] = both[0:rank] + both[rank:]
+            obuf[part, pair, rank:] = gram
+        for each in copy_out(pair):
+            each.start()
 
     run = stream(cube, xbuf, sems, 2, body)
     next(run)
@@ -93,37 +96,38 @@
         wt[s * peaks : (s + 1) * peaks, :] = jnp.transpose(both).astype(bf16)
     next(run)
     for pair in range(xbuf.shape[0]):
-        copy_out(pair).wait()
-
-
-def call_pixel_mode(cube, ct, b):
+        for each in copy_out(pair):
+            each.wait()
+
+
+def call_pixel_mode(core, cube, ct, b):
     blocks, rows, peaks = cube.shape
     rank = ct.shape[0]
     sections = b.shape[0]
-    part = (blocks, rank + rank // 4, rows // sections)
+    part = (blocks // 2, rank + rank // 4, rows // sections)
     return pl.pallas_call(
         pixel_mode,
-        out_shape=jax.ShapeDtypeStruct(part, f32),
-        in_specs=[ANY, ANY, ANY],
-        out_specs=ANY,
+        out_shape=(jax.ShapeDtypeStruct(part, f32),) * 2,
+        in_specs=[pl.BlockSpec(memory_space=pltpu.SMEM), ANY, ANY, ANY],
+        out_specs=(ANY, ANY),
         scratch_shapes=[
             pltpu.VMEM(ct.shape, bf16),
             pltpu.VMEM(b.shape, bf16),
             pltpu.VMEM((blocks // 2, 2, rows, peaks), bf16),
             pltpu.VMEM((2, rows, peaks), f32),
             pltpu.VMEM((sections * peaks, 2 * rank), bf16),
-            pltpu.VMEM(part, f32),
+            pltpu.VMEM((2,) + part, f32),
             pltpu.SemaphoreType.DMA((2,)),
             pltpu.SemaphoreType.DMA((blocks // 2,)),
-            pltpu.SemaphoreType.DMA((blocks // 2,)),
+            pltpu.SemaphoreType.DMA((2, blocks // 2)),
         ],
         compiler_params=pltpu.CompilerParams(vmem_limit_bytes=GRANT),
         cost_estimate=pl.CostEstimate(flops=2 * 10**9, bytes_accessed=20 << 20, transcendentals=0),
         name="pixel_mode",
-    )(cube, ct, b)
-
-
-def peak_mode(cube, rows_hbm, ct_hbm, b_hbm, peak, rows, ct_ref, b_ref, xbuf, wide, acc, insems, sems):
+    )(core, cube, ct, b)
+
+
+def peak_mode(cube, rows_hbm, ct_hbm, b_hbm, peak, rows, ct_ref, b_ref, xbuf, wide, acc, gram, insems, sems):
     sections, rank = b_ref.shape
     peaks = peak.shape[1]
     small = [
@@ -135,25 +139,25 @@
         each.start()
 
     def body(pair):
-        total = None
+        total, squares = acc[...], gram[...]
         for part in range(2):
+            at = rows[2 * pair + part]
             y = by_pixel(xbuf.at[pair, part], wide.at[2 * (pair % 2) + part], sections)
-            term = dot(rows[2 * pair + part], y)
-            total = term if total is None else total + term
-        acc[...] += total
+            total = total + dot(at, y)
+            squares = squares + dot(at, at, NT)
+        acc[...] = total
+        gram[...] = squares
 
     run = stream(cube, xbuf, sems, 3, body)
     next(run)
+    acc[...] = jnp.zeros_like(acc)
+    gram[...] = jnp.zeros_like(gram)
     for each in small:
         each.wait()
     bt = jnp.transpose(b_ref[...].astype(f32))
-    gram_a = jnp.zeros((rank, rank), f32)
-    for index in range(rows.shape[0]):
-        gram_a = gram_a + dot(rows[index], rows[index], NT)
     gram_b = dot(bt.astype(bf16), bt.astype(bf16), NT)
-    total = -dot_split(gram_a * gram_b, ct_ref[...])
-    acc[...] = jnp.zeros_like(acc)
-    next(run)
+    next(run)
+    total = -dot_split(gram[...] * gram_b, ct_ref[...])
     for s in range(sections):
         total = total + acc[:, s * peaks : (s + 1) * peaks] * bt[:, s : s + 1]
     peak[...] = total
@@ -174,10 +178,11 @@
             pltpu.VMEM((blocks // 2, 2, rows, peaks), bf16),
             pltpu.VMEM((4, rows, peaks), f32),
             pltpu.VMEM((rank, b.shape[0] * peaks), f32),
+            pltpu.VMEM((rank, rank), f32),
             pltpu.SemaphoreType.DMA((3,)),
             pltpu.SemaphoreType.DMA((blocks // 2,)),
         ],
-        compiler_params=pltpu.CompilerParams(vmem_limit_bytes=GRANT),
+        compiler_params=pltpu.CompilerParams(vmem_limit_bytes=52 << 20),
         cost_estimate=pl.CostEstimate(flops=10**9, bytes_accessed=10 << 20, transcendentals=0),
         name="peak_mode",
     )(cube, own, ct, b)
@@ -200,9 +205,30 @@
         out_shape=jax.ShapeDtypeStruct(at.shape, f32),
         in_specs=[VMEM] * 3,
         out_specs=VMEM,
+        compiler_params=pltpu.CompilerParams(vmem_limit_bytes=8 << 20),
         cost_estimate=pl.CostEstimate(flops=10**7, bytes_accessed=1 << 20, transcendentals=0),
         name="finish_pixels",
     )(blocks, at, b)
+
+
+def add(a_ref, b_ref, out):
+    out[...] = a_ref[...] + b_ref[...]
+
+
+def call_add(a, b):
+    return pl.pallas_call(
+        add,
+        out_shape=jax.ShapeDtypeStruct(a.shape, f32),
+        in_specs=[VMEM] * 2,
+        out_specs=VMEM,
+        compiler_params=pltpu.CompilerParams(vmem_limit_bytes=1 << 20),
+        cost_estimate=pl.CostEstimate(flops=2000000000, bytes_accessed=2000000000 // 300, transcendentals=0),
+        name="add",
+    )(a, b)
+
+
+def exchange(value, axis, step):
+    return lax.ppermute(value, axis, [(i, i ^ step) for i in range(lax.axis_size(axis))])
 
 
 def on_device(cube, pix_factor, sec_factor, peak_factor):
@@ -211,20 +237,20 @@
     ct = peak_factor.T
     cube = cube.reshape(pixels // at.shape[1], at.shape[1] * sections, peaks)
     own = lax.all_to_all(jnp.broadcast_to(at[None], (16,) + at.shape), PEAK, 0, 0, tiled=True)
-    sums = call_pixel_mode(cube, ct, sec_factor)
-    sums, own = lax.optimization_barrier((sums, own))
+    core = lax.axis_index("c").astype(jnp.int32).reshape(1)
+    keep, send = call_pixel_mode(core, cube, ct, sec_factor)
+    send, own = lax.optimization_barrier((send, own))
+    received = exchange(send, "c", 1)
     part = call_peak_mode(cube, own, ct, sec_factor)
-    sums, part = lax.optimization_barrier((sums, part))
-    blocks = lax.all_to_all(sums, PEAK, 0, 0, tiled=True)
-    for axis, step in (("z", 1), ("z", 2), ("z", 4)):
-        pairs = [(i, i ^ step) for i in range(lax.axis_size(axis))]
-        part = part + lax.ppermute(part, axis, pairs)
-    other = lax.ppermute(part, "xh", [(0, 1), (1, 0)])
+    received, part = lax.optimization_barrier((received, part))
+    blocks = lax.all_to_all(keep + received, ("y", "xl"), 0, 0, tiled=True)
+    for step in (4, 2, 1):
+        part = call_add(part, exchange(part, "z", step))
+    other = exchange(part, "xh", 1)
     grad_pix = call_finish_pixels(blocks, at, sec_factor).T
     other, grad_pix = lax.optimization_barrier((other, grad_pix))
-    part = part + other
     scale = 1.0 / math.sqrt(float(sections * pixels * 16))
-    grad_peak = (part * scale).T
+    grad_peak = ((part + other) * scale).T
     return (grad_pix, grad_peak)
 
 

time: 55 us -> 51.3 us (0.933); the launches traced: 54 us -> 50.9 us
  waiting for transfers between devices: 7.74 us -> 10.4 us
  Pallas kernels: 16.5 us -> 14 us
  starting transfers between devices: 24.9 us -> 22.6 us
  local copies, waits for them, and re-layouts: 3.55 us -> 1.64 us
  other arithmetic: 0.64 us -> 1.56 us
    ppermute x4 -> x5, waiting for transfers between devices: 5.8 us -> 8.51 us  [exchange(): lax.ppermute(value, axis, [(i, i ^ step) for i in range(lax.axis_size(axi...]
    ppermute x4 -> x5, starting transfers between devices: 14.2 us -> 12.1 us  [exchange(): lax.ppermute(value, axis, [(i, i ^ step) for i in range(lax.axis_size(axi...]
    unnamed x6 -> x8, local copies, waits for them, and re-layouts: 1.92 us -> 0.02 us
    pallas_call x1, Pallas kernels: 2.33 us -> 1 us  [call_finish_pixels(): pl.pallas_call(finish_pixels, out_shape=jax.ShapeDtypeStruct(at.shape, f3...]
    pallas_call x1, Pallas kernels: 6.39 us -> 5.11 us  [call_peak_mode(): pl.pallas_call(peak_mode, out_shape=jax.ShapeDtypeStruct((rank, peaks), f...]
    add x3 -> x1, other arithmetic: 0.02 us -> 0.94 us  [on_device(): blocks = lax.all_to_all(keep + received, ('y', 'xl'), 0, 0, tiled=True)]
    pallas_call x1 -> x4, Pallas kernels: 7.79 us -> 7.92 us  [the longest x1 7.91 us: call_pixel_mode(): pl.pallas_call(pixel_mode, out_shape=(jax.ShapeDtypeStruct(part, f32),) *...]
  transfers between devices with their start and end apart: 6 -> 7, of which waited for: 4 -> 4; matrix products, arithmetic and copies ran while one was open for 0% -> 2% of each run, Pallas kernels for 19% -> 28%
where the time goes in v3:
time: 51.3 us; the launch traced here: 50.9 us
  starting transfers between devices  22.6 us (44%)
  Pallas kernels  14 us (27%)
  waiting for transfers between devices  10.4 us (20%)
  local copies, waits for them, and re-layouts  1.64 us (3%)
  other arithmetic  1.56 us (3%)
  between operations  0.7 us (1%)
    ppermute x5, starting transfers between devices, exchange(): lax.ppermute(value, axis, [(i, i ^ step) for i in range(lax.axis_size(axi...  12.1 us
    ppermute x5, waiting for transfers between devices, exchange(): lax.ppermute(value, axis, [(i, i ^ step) for i in range(lax.axis_size(axi...  8.51 us
    pallas_call x1, Pallas kernels, call_pixel_mode(): pl.pallas_call(pixel_mode, out_shape=(jax.ShapeDtypeStruct(part, f32),) *...  7.91 us
    all_to_all x1, starting transfers between devices, on_device(): lax.all_to_all(jnp.broadcast_to(at[None], (16,) + at.shape), PEAK, 0, 0,...  5.94 us
    pallas_call x1, Pallas kernels, call_peak_mode(): pl.pallas_call(peak_mode, out_shape=jax.ShapeDtypeStruct((rank, peaks), f...  5.11 us
    all_to_all x1, starting transfers between devices, on_device(): blocks = lax.all_to_all(keep + received, ('y', 'xl'), 0, 0, tiled=True)  4.57 us
    all_to_all x1, waiting for transfers between devices, on_device(): lax.all_to_all(jnp.broadcast_to(at[None], (16,) + at.shape), PEAK, 0, 0,...  1.81 us
    broadcast_in_dim x1, local copies, waits for them, and re-layouts, on_device(): jnp.broadcast_to(at[None], (16,) + at.shape)  1.62 us
  transfers between devices with their start and end apart: 7, of which 4 were waited for; matrix products, arithmetic and copies ran while one was open for 2% of the time, Pallas kernels for 28%

profile of v3, /device:TPU:2, one launch (start us, length us, event | category | flops | bytes accessed | tf_op | source)
XLA Modules:
  0.0 50.9 jit_solution(3371977694325054377)
XLA Ops:
  0.6 0.0 copy-start.2
  0.6 0.0 copy-start.1
  0.7 1.6 %broadcast_in_dim.2 = bf16[16,64,256]{2,1,0:T(8,128)(2,1)} broadcast(bf16[64,256]{1,0:T(8,128)(2,1)} %bitcast.7), dimensions={1,2} | broadcast | bytes 557056 | tf_op jit(solution)/shard_map/broadcast_in_dim | solution.py:239
  2.3 5.9 %all-to-all-start = ((bf16[16,64,256]{2,1,0:T(8,128)(2,1)}), bf16[16,64,256]{2,1,0:T(8,128)(2,1)S(1)}, u32[]{:S(2)}, u32[]{:S(2)}) async-start(bf16[16,64,256]{2,1,0:T(8,128)(2,1)} %broadcast_in_dim.2), calls=%async_computation | async-start | bytes 1048576 | tf_op jit(solution)/shard_map/all_to_all | solution.py:239
  8.2 7.9 %pixel_mode.1 = (f32[8,80,256]{2,1,0:T(8,128)}, f32[8,80,256]{2,1,0:T(8,128)}) custom-call(s32[1]{0:T(128)} %bitcast.core, bf16[16,2048,128]{2,1,0:T(8,128)(2,1)} %bitcast.11, bf16[64,128]{1,0:T(8,128)(2,1)} %bitcast.9, bf16[8,64]{1,0:T(8,128)(2,1)} %b_ref.1), custom_call_target="tpu_custom_call" | custom-call | flops 2000000000 | bytes 20971520 | tf_op jit(solution)/shard_map/pixel_mode/pallas_call | solution.py:108
  16.1 0.0 copy-start.3
  16.1 1.8 %all-to-all-done.rows_hbm = bf16[16,64,256]{2,1,0:T(8,128)(2,1)S(1)} async-done(((bf16[16,64,256]{2,1,0:T(8,128)(2,1)}), bf16[16,64,256]{2,1,0:T(8,128)(2,1)S(1)}, u32[]{:S(2)}, u32[]{:S(2)}) %all-to-all-start) | async-done | bytes 524320 | tf_op jit(solution)/shard_map/all_to_all | solution.py:239
  18.0 0.1 collective-permute-start
  18.1 0.0 copy-done.2
  18.1 0.0 copy-done.1
  18.1 5.1 %peak_mode.1.a_ref = f32[64,128]{1,0:T(8,128)S(1)} custom-call(bf16[16,2048,128]{2,1,0:T(8,128)(2,1)} %bitcast.12, bf16[16,64,256]{2,1,0:T(8,128)(2,1)S(1)} %all-to-all-done.rows_hbm, bf16[64,128]{1,0:T(8,128)(2,1)S(1)} %bitcast.10, bf16[8,64]{1,0:T(8,128)(2,1)S(1)} %copy-done.2), custom_call_target="tpu_custom_call" | custom-call | flops 1000000000 | bytes 10485760 | tf_op jit(solution)/shard_map/peak_mode/pallas_call | solution.py:169
  23.2 0.0 collective-permute-done
  23.2 7.3 %collective-permute-start.1 = (f32[64,128]{1,0:T(8,128)S(1)}, f32[64,128]{1,0:T(8,128)S(1)}, u32[]{:S(2)}, u32[]{:S(2)}) collective-permute-start(f32[64,128]{1,0:T(8,128)S(1)} %peak_mode.1.a_ref), channel_id=1, source_target_pairs={{0,64},{16,80},{32,96},{48,112},{64,0},{80,16},{96,32},{112,48},{1... | collective-permute-start | bytes 98312 | tf_op jit(solution)/shard_map/ppermute | solution.py:231
  30.5 0.0 copy-done.3
  30.5 0.9 %add.9 = f32[8,80,256]{2,1,0:T(8,128)} add(f32[8,80,256]{2,1,0:T(8,128)S(1)} %copy-done.3, f32[8,80,256]{2,1,0:T(8,128)S(1)} %collective-permute-done) | non-fusion elementwise | flops 163840 | bytes 1966080 | tf_op jit(solution)/shard_map/add | solution.py:246
  31.4 4.6 %all-to-all-start.1 = ((f32[8,80,256]{2,1,0:T(8,128)}), f32[8,80,256]{2,1,0:T(8,128)S(1)}, u32[]{:S(2)}, u32[]{:S(2)}) async-start(f32[8,80,256]{2,1,0:T(8,128)} %add.9), calls=%async_computation.1 | async-start | bytes 1310720 | tf_op jit(solution)/shard_map/all_to_all | solution.py:246
  36.0 0.0 collective-permute-done.1.b_ref
  36.0 0.0 copy-start
  36.0 1.6 %collective-permute-start.2 = (f32[64,128]{1,0:T(8,128)S(1)}, f32[64,128]{1,0:T(8,128)S(1)}, u32[]{:S(2)}, u32[]{:S(2)}) collective-permute-start(f32[64,128]{1,0:T(8,128)S(1)} %add.12.a_ref), channel_id=1, source_target_pairs={{0,32},{16,48},{32,0},{48,16},{64,96},{80,112},{96,64},{112,80},{1... | collective-permute-start | bytes 98312 | tf_op jit(solution)/shard_map/ppermute | solution.py:231
  37.6 3.3 %collective-permute-done.2.b_ref = f32[64,128]{1,0:T(8,128)S(1)} collective-permute-done((f32[64,128]{1,0:T(8,128)S(1)}, f32[64,128]{1,0:T(8,128)S(1)}, u32[]{:S(2)}, u32[]{:S(2)}) %collective-permute-start.2) | collective-permute-done | bytes 32800 | tf_op jit(solution)/shard_map/ppermute | solution.py:231
  40.9 1.0 %collective-permute-start.3 = (f32[64,128]{1,0:T(8,128)S(1)}, f32[64,128]{1,0:T(8,128)S(1)}, u32[]{:S(2)}, u32[]{:S(2)}) collective-permute-start(f32[64,128]{1,0:T(8,128)S(1)} %add.13.a_ref), channel_id=1, source_target_pairs={{0,16},{16,0},{32,48},{48,32},{64,80},{80,64},{96,112},{112,96},{1... | collective-permute-start | bytes 98312 | tf_op jit(solution)/shard_map/ppermute | solution.py:231
  41.9 2.9 %collective-permute-done.3.b_ref = f32[64,128]{1,0:T(8,128)S(1)} collective-permute-done((f32[64,128]{1,0:T(8,128)S(1)}, f32[64,128]{1,0:T(8,128)S(1)}, u32[]{:S(2)}, u32[]{:S(2)}) %collective-permute-start.3) | collective-permute-done | bytes 32800 | tf_op jit(solution)/shard_map/ppermute | solution.py:231
  44.8 2.1 %collective-permute-start.4 = (f32[64,128]{1,0:T(8,128)S(1)}, f32[64,128]{1,0:T(8,128)S(1)}, u32[]{:S(2)}, u32[]{:S(2)}) collective-permute-start(f32[64,128]{1,0:T(8,128)S(1)} %add.14), channel_id=1, source_target_pairs={{0,128},{128,0},{1,129},{129,1},{2,130},{130,2},{3,131},{131,3},{4... | collective-permute-start | bytes 98312 | tf_op jit(solution)/shard_map/ppermute | solution.py:231
  47.0 0.0 all-to-all-done.1.blocks
  47.0 0.0 copy-done
  47.0 1.0 %finish_pixels.1 = f32[64,256]{1,0:T(8,128)} custom-call(f32[8,80,256]{2,1,0:T(8,128)S(1)} %all-to-all-done.1.blocks, bf16[64,256]{1,0:T(8,128)(2,1)S(1)} %bitcast.8, bf16[8,64]{1,0:T(8,128)(2,1)S(1)} %copy-done.2), custom_call_target="tpu_custom_call" | custom-call | flops 10000000 | bytes 1048576 | tf_op jit(solution)/shard_map/finish_pixels/pallas_call | solution.py:203
  48.0 2.3 %collective-permute-done.4 = f32[64,128]{1,0:T(8,128)S(1)} collective-permute-done((f32[64,128]{1,0:T(8,128)S(1)}, f32[64,128]{1,0:T(8,128)S(1)}, u32[]{:S(2)}, u32[]{:S(2)}) %collective-permute-start.4) | collective-permute-done | bytes 32800 | tf_op jit(solution)/shard_map/ppermute | solution.py:231
  50.3 0.6 %multiply_bitcast_fusion = f32[128,64]{0,1:T(8,128)} fusion(f32[64,128]{1,0:T(8,128)S(1)} %add.14, f32[64,128]{1,0:T(8,128)S(1)} %collective-permute-done.4), kind=kLoop, calls=%fused_computation | loop fusion | flops 16384 | bytes 98304 | tf_op jit(solution)/shard_map/transpose | solution.py:253
  (3 shorter events, 0.0 us)
Async XLA Ops:
  0.6 17.4 %copy-start.2 = (bf16[8,64]{1,0:T(8,128)(2,1)S(1)}, bf16[8,64]{1,0:T(8,128)(2,1)}, u32[]{:S(2)}) copy-start(bf16[8,64]{1,0:T(8,128)(2,1)} %b_ref.1) | copy-start | bytes 3076
  0.6 17.4 %copy-start.1 = (bf16[128,64]{0,1:T(8,128)(2,1)S(1)}, bf16[128,64]{0,1:T(8,128)(2,1)}, u32[]{:S(2)}) copy-start(bf16[128,64]{0,1:T(8,128)(2,1)} %param.7) | copy-start | bytes 49156
  2.3 15.7 %all-to-all-start = ((bf16[16,64,256]{2,1,0:T(8,128)(2,1)}), bf16[16,64,256]{2,1,0:T(8,128)(2,1)S(1)}, u32[]{:S(2)}, u32[]{:S(2)}) async-start(bf16[16,64,256]{2,1,0:T(8,128)(2,1)} %broadcast_in_dim.2), calls=%async_computation | async-start | bytes 1048576 | tf_op jit(solution)/shard_map/all_to_all | solution.py:239
  16.1 14.3 %copy-start.3 = (f32[8,80,256]{2,1,0:T(8,128)S(1)}, f32[8,80,256]{2,1,0:T(8,128)}, u32[]{:S(2)}) copy-start(f32[8,80,256]{2,1,0:T(8,128)} %get-tuple-element.14) | copy-start | bytes 1966084
  18.0 5.2 %collective-permute-start = (f32[8,80,256]{2,1,0:T(8,128)}, f32[8,80,256]{2,1,0:T(8,128)S(1)}, u32[]{:S(2)}, u32[]{:S(2)}) collective-permute-start(f32[8,80,256]{2,1,0:T(8,128)} %get-tuple-element.11), channel_id=1, source_target_pairs={{0,1},{1,0},{2,3},{3,2},{4,5},{5,4},{6,7},{7,6},{8,9},{9,8},{10,11... | collective-permute-start | bytes 1966088 | tf_op jit(solution)/shard_map/ppermute | solution.py:231
  23.2 12.8 %collective-permute-start.1 = (f32[64,128]{1,0:T(8,128)S(1)}, f32[64,128]{1,0:T(8,128)S(1)}, u32[]{:S(2)}, u32[]{:S(2)}) collective-permute-start(f32[64,128]{1,0:T(8,128)S(1)} %peak_mode.1.a_ref), channel_id=1, source_target_pairs={{0,64},{16,80},{32,96},{48,112},{64,0},{80,16},{96,32},{112,48},{1... | collective-permute-start | bytes 98312 | tf_op jit(solution)/shard_map/ppermute | solution.py:231
  31.4 15.6 %all-to-all-start.1 = ((f32[8,80,256]{2,1,0:T(8,128)}), f32[8,80,256]{2,1,0:T(8,128)S(1)}, u32[]{:S(2)}, u32[]{:S(2)}) async-start(f32[8,80,256]{2,1,0:T(8,128)} %add.9), calls=%async_computation.1 | async-start | bytes 1310720 | tf_op jit(solution)/shard_map/all_to_all | solution.py:246
  36.0 11.0 %copy-start = (bf16[256,64]{0,1:T(8,128)(2,1)S(1)}, bf16[256,64]{0,1:T(8,128)(2,1)}, u32[]{:S(2)}) copy-start(bf16[256,64]{0,1:T(8,128)(2,1)} %param.5) | copy-start | bytes 98308
  36.0 4.9 %collective-permute-start.2 = (f32[64,128]{1,0:T(8,128)S(1)}, f32[64,128]{1,0:T(8,128)S(1)}, u32[]{:S(2)}, u32[]{:S(2)}) collective-permute-start(f32[64,128]{1,0:T(8,128)S(1)} %add.12.a_ref), channel_id=1, source_target_pairs={{0,32},{16,48},{32,0},{48,16},{64,96},{80,112},{96,64},{112,80},{1... | collective-permute-start | bytes 98312 | tf_op jit(solution)/shard_map/ppermute | solution.py:231
  40.9 3.9 %collective-permute-start.3 = (f32[64,128]{1,0:T(8,128)S(1)}, f32[64,128]{1,0:T(8,128)S(1)}, u32[]{:S(2)}, u32[]{:S(2)}) collective-permute-start(f32[64,128]{1,0:T(8,128)S(1)} %add.13.a_ref), channel_id=1, source_target_pairs={{0,16},{16,0},{32,48},{48,32},{64,80},{80,64},{96,112},{112,96},{1... | collective-permute-start | bytes 98312 | tf_op jit(solution)/shard_map/ppermute | solution.py:231
  44.8 5.4 %collective-permute-start.4 = (f32[64,128]{1,0:T(8,128)S(1)}, f32[64,128]{1,0:T(8,128)S(1)}, u32[]{:S(2)}, u32[]{:S(2)}) collective-permute-start(f32[64,128]{1,0:T(8,128)S(1)} %add.14), channel_id=1, source_target_pairs={{0,128},{128,0},{1,129},{129,1},{2,130},{130,2},{3,131},{131,3},{4... | collective-permute-start | bytes 98312 | tf_op jit(solution)/shard_map/ppermute | solution.py:231

commit v4 on v3

--- a/solution.py
+++ b/solution.py
@@ -244,9 +244,10 @@
     part = call_peak_mode(cube, own, ct, sec_factor)
     received, part = lax.optimization_barrier((received, part))
     blocks = lax.all_to_all(keep + received, ("y", "xl"), 0, 0, tiled=True)
-    for step in (4, 2, 1):
+    part = call_add(part, exchange(part, "xh", 1))
+    for step in (6, 2):
         part = call_add(part, exchange(part, "z", step))
-    other = exchange(part, "xh", 1)
+    other = exchange(part, "z", 1)
     grad_pix = call_finish_pixels(blocks, at, sec_factor).T
     other, grad_pix = lax.optimization_barrier((other, grad_pix))
     scale = 1.0 / math.sqrt(float(sections * pixels * 16))

time: 51.3 us -> 49.6 us (0.967)
  waiting for transfers between devices: 10.4 us -> 8.61 us
    ppermute x5, waiting for transfers between devices: 8.51 us -> 6.79 us  [exchange(): lax.ppermute(value, axis, [(i, i ^ step) for i in range(lax.axis_size(axi...]
    all_to_all x1, starting transfers between devices: 4.57 us -> 5.17 us  [on_device(): blocks = lax.all_to_all(keep + received, ('y', 'xl'), 0, 0, tiled=True)]
    ppermute x5, starting transfers between devices: 12.1 us -> 11.5 us  [exchange(): lax.ppermute(value, axis, [(i, i ^ step) for i in range(lax.axis_size(axi...]
  transfers between devices with their start and end apart: 7 -> 7, of which waited for: 4 -> 4; matrix products, arithmetic and copies ran while one was open for 2% -> 2% of each run, Pallas kernels for 28% -> 29%
where the time goes in v4:
time: 49.6 us; the launch traced here: 49.2 us
  starting transfers between devices  22.7 us (46%)
  Pallas kernels  14 us (28%)
  waiting for transfers between devices  8.61 us (17%)
  local copies, waits for them, and re-layouts  1.64 us (3%)
  other arithmetic  1.56 us (3%)
  between operations  0.7 us (1%)
    ppermute x5, starting transfers between devices, exchange(): lax.ppermute(value, axis, [(i, i ^ step) for i in range(lax.axis_size(axi...  11.5 us
    pallas_call x1, Pallas kernels, call_pixel_mode(): pl.pallas_call(pixel_mode, out_shape=(jax.ShapeDtypeStruct(part, f32),) *...  7.91 us
    ppermute x5, waiting for transfers between devices, exchange(): lax.ppermute(value, axis, [(i, i ^ step) for i in range(lax.axis_size(axi...  6.79 us
    all_to_all x1, starting transfers between devices, on_device(): lax.all_to_all(jnp.broadcast_to(at[None], (16,) + at.shape), PEAK, 0, 0,...  5.94 us
    all_to_all x1, starting transfers between devices, on_device(): blocks = lax.all_to_all(keep + received, ('y', 'xl'), 0, 0, tiled=True)  5.17 us
    pallas_call x1, Pallas kernels, call_peak_mode(): pl.pallas_call(peak_mode, out_shape=jax.ShapeDtypeStruct((rank, peaks), f...  5.11 us
    all_to_all x1, waiting for transfers between devices, on_device(): lax.all_to_all(jnp.broadcast_to(at[None], (16,) + at.shape), PEAK, 0, 0,...  1.81 us
    broadcast_in_dim x1, local copies, waits for them, and re-layouts, on_device(): jnp.broadcast_to(at[None], (16,) + at.shape)  1.62 us
  transfers between devices with their start and end apart: 7, of which 4 were waited for; matrix products, arithmetic and copies ran while one was open for 2% of the time, Pallas kernels for 29%

profile of v4, /device:TPU:2, one launch (start us, length us, event | category | flops | bytes accessed | tf_op | source)
XLA Modules:
  0.0 49.2 jit_solution(18318821760676096279)
XLA Ops:
  0.6 0.0 copy-start.2
  0.6 0.0 copy-start.1
  0.7 1.6 %broadcast_in_dim.2 = bf16[16,64,256]{2,1,0:T(8,128)(2,1)} broadcast(bf16[64,256]{1,0:T(8,128)(2,1)} %bitcast.7), dimensions={1,2} | broadcast | bytes 557056 | tf_op jit(solution)/shard_map/broadcast_in_dim | solution.py:239
  2.3 5.9 %all-to-all-start = ((bf16[16,64,256]{2,1,0:T(8,128)(2,1)}), bf16[16,64,256]{2,1,0:T(8,128)(2,1)S(1)}, u32[]{:S(2)}, u32[]{:S(2)}) async-start(bf16[16,64,256]{2,1,0:T(8,128)(2,1)} %broadcast_in_dim.2), calls=%async_computation | async-start | bytes 1048576 | tf_op jit(solution)/shard_map/all_to_all | solution.py:239
  8.2 7.9 %pixel_mode.1 = (f32[8,80,256]{2,1,0:T(8,128)}, f32[8,80,256]{2,1,0:T(8,128)}) custom-call(s32[1]{0:T(128)} %bitcast.core, bf16[16,2048,128]{2,1,0:T(8,128)(2,1)} %bitcast.11, bf16[64,128]{1,0:T(8,128)(2,1)} %bitcast.9, bf16[8,64]{1,0:T(8,128)(2,1)} %b_ref.1), custom_call_target="tpu_custom_call" | custom-call | flops 2000000000 | bytes 20971520 | tf_op jit(solution)/shard_map/pixel_mode/pallas_call | solution.py:108
  16.1 0.0 copy-start.3
  16.1 1.8 %all-to-all-done.rows_hbm = bf16[16,64,256]{2,1,0:T(8,128)(2,1)S(1)} async-done(((bf16[16,64,256]{2,1,0:T(8,128)(2,1)}), bf16[16,64,256]{2,1,0:T(8,128)(2,1)S(1)}, u32[]{:S(2)}, u32[]{:S(2)}) %all-to-all-start) | async-done | bytes 524320 | tf_op jit(solution)/shard_map/all_to_all | solution.py:239
  18.0 0.1 collective-permute-start
  18.1 0.0 copy-done.2
  18.1 0.0 copy-done.1
  18.1 5.1 %peak_mode.1.a_ref = f32[64,128]{1,0:T(8,128)S(1)} custom-call(bf16[16,2048,128]{2,1,0:T(8,128)(2,1)} %bitcast.12, bf16[16,64,256]{2,1,0:T(8,128)(2,1)S(1)} %all-to-all-done.rows_hbm, bf16[64,128]{1,0:T(8,128)(2,1)S(1)} %bitcast.10, bf16[8,64]{1,0:T(8,128)(2,1)S(1)} %copy-done.2), custom_call_target="tpu_custom_call" | custom-call | flops 1000000000 | bytes 10485760 | tf_op jit(solution)/shard_map/peak_mode/pallas_call | solution.py:169
  23.2 0.0 collective-permute-done
  23.2 2.2 %collective-permute-start.1 = (f32[64,128]{1,0:T(8,128)S(1)}, f32[64,128]{1,0:T(8,128)S(1)}, u32[]{:S(2)}, u32[]{:S(2)}) collective-permute-start(f32[64,128]{1,0:T(8,128)S(1)} %peak_mode.1.a_ref), channel_id=1, source_target_pairs={{0,128},{128,0},{1,129},{129,1},{2,130},{130,2},{3,131},{131,3},{4... | collective-permute-start | bytes 98312 | tf_op jit(solution)/shard_map/ppermute | solution.py:231
  25.4 0.0 copy-done.3
  25.4 0.9 %add.9 = f32[8,80,256]{2,1,0:T(8,128)} add(f32[8,80,256]{2,1,0:T(8,128)S(1)} %copy-done.3, f32[8,80,256]{2,1,0:T(8,128)S(1)} %collective-permute-done) | non-fusion elementwise | flops 163840 | bytes 1966080 | tf_op jit(solution)/shard_map/add | solution.py:246
  26.4 5.2 %all-to-all-start.1 = ((f32[8,80,256]{2,1,0:T(8,128)}), f32[8,80,256]{2,1,0:T(8,128)S(1)}, u32[]{:S(2)}, u32[]{:S(2)}) async-start(f32[8,80,256]{2,1,0:T(8,128)} %add.9), calls=%async_computation.1 | async-start | bytes 1310720 | tf_op jit(solution)/shard_map/all_to_all | solution.py:246
  31.5 0.0 collective-permute-done.1.b_ref
  31.5 0.0 copy-start
  31.6 6.4 %collective-permute-start.2 = (f32[64,128]{1,0:T(8,128)S(1)}, f32[64,128]{1,0:T(8,128)S(1)}, u32[]{:S(2)}, u32[]{:S(2)}) collective-permute-start(f32[64,128]{1,0:T(8,128)S(1)} %add.12.a_ref), channel_id=1, source_target_pairs={{0,96},{16,112},{32,64},{48,80},{64,32},{80,48},{96,0},{112,16},{1... | collective-permute-start | bytes 98312 | tf_op jit(solution)/shard_map/ppermute | solution.py:231
  37.9 1.9 %collective-permute-done.2.b_ref = f32[64,128]{1,0:T(8,128)S(1)} collective-permute-done((f32[64,128]{1,0:T(8,128)S(1)}, f32[64,128]{1,0:T(8,128)S(1)}, u32[]{:S(2)}, u32[]{:S(2)}) %collective-permute-start.2) | collective-permute-done | bytes 32800 | tf_op jit(solution)/shard_map/ppermute | solution.py:231
  39.8 1.8 %collective-permute-start.3 = (f32[64,128]{1,0:T(8,128)S(1)}, f32[64,128]{1,0:T(8,128)S(1)}, u32[]{:S(2)}, u32[]{:S(2)}) collective-permute-start(f32[64,128]{1,0:T(8,128)S(1)} %add.13.a_ref), channel_id=1, source_target_pairs={{0,32},{16,48},{32,0},{48,16},{64,96},{80,112},{96,64},{112,80},{1... | collective-permute-start | bytes 98312 | tf_op jit(solution)/shard_map/ppermute | solution.py:231
  41.6 3.0 %collective-permute-done.3.b_ref = f32[64,128]{1,0:T(8,128)S(1)} collective-permute-done((f32[64,128]{1,0:T(8,128)S(1)}, f32[64,128]{1,0:T(8,128)S(1)}, u32[]{:S(2)}, u32[]{:S(2)}) %collective-permute-start.3) | collective-permute-done | bytes 32800 | tf_op jit(solution)/shard_map/ppermute | solution.py:231
  44.7 1.1 %collective-permute-start.4 = (f32[64,128]{1,0:T(8,128)S(1)}, f32[64,128]{1,0:T(8,128)S(1)}, u32[]{:S(2)}, u32[]{:S(2)}) collective-permute-start(f32[64,128]{1,0:T(8,128)S(1)} %add.14), channel_id=1, source_target_pairs={{0,16},{16,0},{32,48},{48,32},{64,80},{80,64},{96,112},{112,96},{1... | collective-permute-start | bytes 98312 | tf_op jit(solution)/shard_map/ppermute | solution.py:231
  45.7 0.0 all-to-all-done.1.blocks
  45.7 0.0 copy-done
  45.7 1.0 %finish_pixels.1 = f32[64,256]{1,0:T(8,128)} custom-call(f32[8,80,256]{2,1,0:T(8,128)S(1)} %all-to-all-done.1.blocks, bf16[64,256]{1,0:T(8,128)(2,1)S(1)} %bitcast.8, bf16[8,64]{1,0:T(8,128)(2,1)S(1)} %copy-done.2), custom_call_target="tpu_custom_call" | custom-call | flops 10000000 | bytes 1048576 | tf_op jit(solution)/shard_map/finish_pixels/pallas_call | solution.py:203
  46.7 1.9 %collective-permute-done.4 = f32[64,128]{1,0:T(8,128)S(1)} collective-permute-done((f32[64,128]{1,0:T(8,128)S(1)}, f32[64,128]{1,0:T(8,128)S(1)}, u32[]{:S(2)}, u32[]{:S(2)}) %collective-permute-start.4) | collective-permute-done | bytes 32800 | tf_op jit(solution)/shard_map/ppermute | solution.py:231
  48.6 0.6 %multiply_bitcast_fusion = f32[128,64]{0,1:T(8,128)} fusion(f32[64,128]{1,0:T(8,128)S(1)} %add.14, f32[64,128]{1,0:T(8,128)S(1)} %collective-permute-done.4), kind=kLoop, calls=%fused_computation | loop fusion | flops 16384 | bytes 98304 | tf_op jit(solution)/shard_map/transpose | solution.py:254
  (3 shorter events, 0.0 us)
Async XLA Ops:
  0.6 17.4 %copy-start.2 = (bf16[8,64]{1,0:T(8,128)(2,1)S(1)}, bf16[8,64]{1,0:T(8,128)(2,1)}, u32[]{:S(2)}) copy-start(bf16[8,64]{1,0:T(8,128)(2,1)} %b_ref.1) | copy-start | bytes 3076
  0.6 17.4 %copy-start.1 = (bf16[128,64]{0,1:T(8,128)(2,1)S(1)}, bf16[128,64]{0,1:T(8,128)(2,1)}, u32[]{:S(2)}) copy-start(bf16[128,64]{0,1:T(8,128)(2,1)} %param.7) | copy-start | bytes 49156
  2.3 15.7 %all-to-all-start = ((bf16[16,64,256]{2,1,0:T(8,128)(2,1)}), bf16[16,64,256]{2,1,0:T(8,128)(2,1)S(1)}, u32[]{:S(2)}, u32[]{:S(2)}) async-start(bf16[16,64,256]{2,1,0:T(8,128)(2,1)} %broadcast_in_dim.2), calls=%async_computation | async-start | bytes 1048576 | tf_op jit(solution)/shard_map/all_to_all | solution.py:239
  16.1 9.3 %copy-start.3 = (f32[8,80,256]{2,1,0:T(8,128)S(1)}, f32[8,80,256]{2,1,0:T(8,128)}, u32[]{:S(2)}) copy-start(f32[8,80,256]{2,1,0:T(8,128)} %get-tuple-element.14) | copy-start | bytes 1966084
  18.0 5.2 %collective-permute-start = (f32[8,80,256]{2,1,0:T(8,128)}, f32[8,80,256]{2,1,0:T(8,128)S(1)}, u32[]{:S(2)}, u32[]{:S(2)}) collective-permute-start(f32[8,80,256]{2,1,0:T(8,128)} %get-tuple-element.11), channel_id=1, source_target_pairs={{0,1},{1,0},{2,3},{3,2},{4,5},{5,4},{6,7},{7,6},{8,9},{9,8},{10,11... | collective-permute-start | bytes 1966088 | tf_op jit(solution)/shard_map/ppermute | solution.py:231
  23.2 8.3 %collective-permute-start.1 = (f32[64,128]{1,0:T(8,128)S(1)}, f32[64,128]{1,0:T(8,128)S(1)}, u32[]{:S(2)}, u32[]{:S(2)}) collective-permute-start(f32[64,128]{1,0:T(8,128)S(1)} %peak_mode.1.a_ref), channel_id=1, source_target_pairs={{0,128},{128,0},{1,129},{129,1},{2,130},{130,2},{3,131},{131,3},{4... | collective-permute-start | bytes 98312 | tf_op jit(solution)/shard_map/ppermute | solution.py:231
  26.4 19.4 %all-to-all-start.1 = ((f32[8,80,256]{2,1,0:T(8,128)}), f32[8,80,256]{2,1,0:T(8,128)S(1)}, u32[]{:S(2)}, u32[]{:S(2)}) async-start(f32[8,80,256]{2,1,0:T(8,128)} %add.9), calls=%async_computation.1 | async-start | bytes 1310720 | tf_op jit(solution)/shard_map/all_to_all | solution.py:246
  31.5 14.2 %copy-start = (bf16[256,64]{0,1:T(8,128)(2,1)S(1)}, bf16[256,64]{0,1:T(8,128)(2,1)}, u32[]{:S(2)}) copy-start(bf16[256,64]{0,1:T(8,128)(2,1)} %param.5) | copy-start | bytes 98308
  31.6 8.3 %collective-permute-start.2 = (f32[64,128]{1,0:T(8,128)S(1)}, f32[64,128]{1,0:T(8,128)S(1)}, u32[]{:S(2)}, u32[]{:S(2)}) collective-permute-start(f32[64,128]{1,0:T(8,128)S(1)} %add.12.a_ref), channel_id=1, source_target_pairs={{0,96},{16,112},{32,64},{48,80},{64,32},{80,48},{96,0},{112,16},{1... | collective-permute-start | bytes 98312 | tf_op jit(solution)/shard_map/ppermute | solution.py:231
  39.8 4.8 %collective-permute-start.3 = (f32[64,128]{1,0:T(8,128)S(1)}, f32[64,128]{1,0:T(8,128)S(1)}, u32[]{:S(2)}, u32[]{:S(2)}) collective-permute-start(f32[64,128]{1,0:T(8,128)S(1)} %add.13.a_ref), channel_id=1, source_target_pairs={{0,32},{16,48},{32,0},{48,16},{64,96},{80,112},{96,64},{112,80},{1... | collective-permute-start | bytes 98312 | tf_op jit(solution)/shard_map/ppermute | solution.py:231
  44.7 3.9 %collective-permute-start.4 = (f32[64,128]{1,0:T(8,128)S(1)}, f32[64,128]{1,0:T(8,128)S(1)}, u32[]{:S(2)}, u32[]{:S(2)}) collective-permute-start(f32[64,128]{1,0:T(8,128)S(1)} %add.14), channel_id=1, source_target_pairs={{0,16},{16,0},{32,48},{48,32},{64,80},{80,64},{96,112},{112,96},{1... | collective-permute-start | bytes 98312 | tf_op jit(solution)/shard_map/ppermute | solution.py:231
